TPU v7x, 32 devices: a whole 2x2x4 slice. The times are simulated.
32 devices in a mesh: gz: 8 (over z, y), gy: 4 (over x, core).
Axes of the slice: x: 2, y: 2, z: 4, core: 2. Of those that a mesh axis runs over, the one named last changes fastest.
Arguments:
- phase: float32 [32, 128, 768], P('gz', 'gy'), may hold values from 0 to 1
- solute: float32 [32, 128, 768], P('gz', 'gy'), may hold values from -0.5 to 0.5
- labels: int32 [32, 128, 768], P('gz', 'gy'), may hold values from 0 to 31
- quat_table: float32 [32, 4], replicated, may hold values from -3 to 3
- heat_map: float32 [128, 768], P('gy'), may hold values from -4 to 4
- cotangent: float32 [6, 32, 128, 768], P(None, 'gz', 'gy'), may hold values from -6 to 6
Outputs:
- final_fields: float32 [6, 32, 128, 768], P(None, 'gz', 'gy')
- sensitivity: float32 [128, 768], P('gy')
- objective: float32 [], replicated
All inputs are finite; a program needn't handle non-finite values.
Results may differ from a plain program's by a relative error of at most 0.0003.
Values sent between devices are 32-bit elements; how exact they have to be, the bound alone decides.
A program may use at most 128 MiB of HBM per device.

v0:
```python
import jax
import jax.numpy as jnp
from jax import lax
from jax.sharding import PartitionSpec as P

time_step = 0.08
drive_gain = 0.6
misfit_gain = 0.2
solute_diff = 0.8
reject_gain = 0.5
solute_shift = 0.5


def padded_2(cells, sides, width):
    for axis, dim in sides:
        count = lax.axis_size(axis)
        head = lax.slice_in_dim(cells, 0, width, axis=dim)
        tail = lax.slice_in_dim(cells, cells.shape[dim] - width, cells.shape[dim], axis=dim)
        cells = jnp.concatenate(
            [
                lax.ppermute(tail, axis, [(i, (i + 1) % count) for i in range(count)]),
                cells,
                lax.ppermute(head, axis, [((i + 1) % count, i) for i in range(count)]),
            ],
            axis=dim,
        )
    return cells


def advance(padded, heat_rows):
    center = padded[:, 1:-1, 1:-1, :]
    border = jnp.zeros_like(center[..., :1])
    laplace = (
        padded[:, 2:, 1:-1, :]
        + padded[:, :-2, 1:-1, :]
        + padded[:, 1:-1, 2:, :]
        + padded[:, 1:-1, :-2, :]
        + jnp.concatenate([center[..., 1:], border], -1)
        + jnp.concatenate([border, center[..., :-1]], -1)
        - 6.0 * center
    )
    phase_now = center[0]
    quaternions = center[1:5]
    solute_now = center[5]
    undercool = heat_rows[None] - solute_shift * solute_now
    misfit = jnp.sum(quaternions * laplace[1:5], axis=0)
    phase_next = phase_now + time_step * (
        laplace[0]
        + 4.0 * phase_now * (1.0 - phase_now) * (phase_now - 0.5 + drive_gain * jnp.tanh(undercool))
        + misfit_gain * phase_now * misfit
    )
    quat_next = quaternions + time_step * ((1.0 - phase_now) ** 2 + 0.1) * laplace[1:5]
    solute_next = (
        solute_now
        + time_step * solute_diff * laplace[5]
        + reject_gain * (phase_next - phase_now) * solute_now
    )
    return jnp.concatenate([phase_next[None], quat_next, solute_next[None]], 0)


def expand_labels(grain_ids, quat_table):
    total = jnp.zeros((4,) + grain_ids.shape, jnp.float32)
    for grain in range(quat_table.shape[0]):
        total = total + jnp.where(
            grain_ids[None] == grain, quat_table[grain][:, None, None, None], 0.0
        )
    return total


def clear_rows(padded, width, low_edge, high_edge):
    rows = jnp.arange(padded.shape[2])
    dropped = (rows < width) & low_edge | (rows >= padded.shape[2] - width) & high_edge
    return jnp.where(dropped[None, None, :, None], 0.0, padded)


def cycle_total(partial_value):
    return lax.psum(partial_value, "gz")


def on_device(phase, solute, labels, quat_table, heat_map, cotangent):
    gy_index = lax.axis_index("gy")
    low_edge = gy_index == 0
    high_edge = gy_index == lax.axis_size("gy") - 1
    stored = []
    fields_first = jnp.concatenate(
        [phase[None], expand_labels(labels, quat_table), solute[None]], 0
    )
    padded = clear_rows(padded_2(fields_first, (("gz", 1), ("gy", 2)), 1), 1, low_edge, high_edge)
    stored.append(padded)
    fields_now = advance(padded, heat_map)
    padded = clear_rows(padded_2(fields_now, (("gz", 1), ("gy", 2)), 1), 1, low_edge, high_edge)
    stored.append(padded)
    fields_now = advance(padded, heat_map)
    objective = lax.psum(jnp.sum(cotangent * fields_now), ("gz", "gy"))
    last_pull = jax.vjp(advance, stored[1], heat_map)[1]
    grad_padded, grad_map_late = last_pull(cotangent)
    summed_late = cycle_total(grad_map_late)
    received = padded_2(grad_padded, (("gz", 1), ("gy", 2)), 1)
    low_keep = jnp.where(low_edge, 0.0, 1.0)
    high_keep = jnp.where(high_edge, 0.0, 1.0)
    adjoint = grad_padded[:, 1:-1, 1:-1, :]
    adjoint = adjoint.at[:, 0].add(received[:, 0, 2:-2, :])
    adjoint = adjoint.at[:, -1].add(received[:, -1, 2:-2, :])
    adjoint = adjoint.at[:, :, 0].add(low_keep * received[:, 2:-2, 0, :])
    adjoint = adjoint.at[:, :, -1].add(high_keep * received[:, 2:-2, -1, :])
    first_stored = stored[0]
    first_pull = jax.vjp(lambda heat: advance(first_stored, heat), heat_map)[1]
    grad_map_early = first_pull(adjoint)[0]
    sensitivity = summed_late + cycle_total(grad_map_early)
    return (fields_now, sensitivity, objective)


def solution(mesh):
    placed = (
        P("gz", "gy", None),
        P("gz", "gy", None),
        P("gz", "gy", None),
        P(),
        P("gy", None),
        P(None, "gz", "gy", None),
    )
    return jax.shard_map(
        on_device,
        mesh=mesh,
        in_specs=placed,
        out_specs=(P(None, "gz", "gy", None), P("gy", None), P()),
        check_vma=False,
    )
```

profile of v0, /device:TPU:1, one launch (start us, length us, event | category | flops | bytes accessed | tf_op | source)
XLA Modules:
  0.0 241.9 jit_solution(5796627415855076050)
XLA Ops:
  10.7 3.4 %broadcast_compare_fusion.31 = (pred[4,32,768]{2,1,0:T(8,128)(4,1)S(1)}, pred[4,32,768]{2,1,0:T(8,128)(4,1)S(1)}, pred[4,32,768]{2,1,0:T(8,128)(4,1)S(1)}, pred[...) fusion(s32[4,32,768]{2,1,0:T(8,128)} %param.16), kind=kLoop, calls=%fused_computation.127 | loop fusion | flops 3145728 | bytes 3538944 | tf_op jit(solution)/shard_map/eq | solution.py:65
  14.1 5.4 %select_add_fusion = f32[4,4,32,768]{3,2,1,0:T(8,128)S(1)} fusion(f32[4]{0:T(128)S(1)} %get-tuple-element.88, f32[4]{0:T(128)S(1)} %get-tuple-element.89, f32[4]{0:T(128)S(1)} %get-tuple-element.59, f32[4]{0:T(128)S(1)} %get-tuple-element.60, f32[4]{0:T(128)S(1)} %get-tuple-element.61, f32[4]{0:T(128)S(1)} %get-tuple-element.62, f32[4]{0:T(128)S(1)} %get-tuple-element.63, ...), kind=kLoop, calls=%fused_computation.27 | loop fusion | flops 24772608 | bytes 4719104 | tf_op jit(solution)/shard_map/add | solution.py:64
  20.6 2.1 collective-permute-start
  22.7 3.0 %collective-permute-start.1 = (f32[6,1,32,768]{3,2,1,0:T(8,128)}, f32[6,1,32,768]{3,2,1,0:T(8,128)S(1)}, u32[]{:S(2)}, u32[]{:S(2)}) collective-permute-start(f32[6,1,32,768]{3,2,1,0:T(8,128)} %get-tuple-element.122), channel_id=1, source_target_pairs={{4,0},{8,4},{12,8},{16,12},{20,16},{24,20},{28,24},{0,28},{5,1},{9... | collective-permute-start | bytes 1769480 | tf_op jit(solution)/shard_map/ppermute | solution.py:23
  25.8 21.9 %collective-permute-done = f32[6,1,32,768]{3,2,1,0:T(8,128)S(1)} collective-permute-done((f32[6,1,32,768]{3,2,1,0:T(8,128)}, f32[6,1,32,768]{3,2,1,0:T(8,128)S(1)}, u32[]{:S(2)}, u32[]{:S(2)}) %collective-permute-start) | collective-permute-done | bytes 589856 | tf_op jit(solution)/shard_map/ppermute | solution.py:21
  49.6 3.0 %collective-permute-start.2 = (f32[6,6,1,768]{3,2,1,0:T(1,128)S(1)}, f32[6,6,1,768]{3,2,1,0:T(1,128)S(1)}, u32[]{:S(2)}, u32[]{:S(2)}) collective-permute-start(f32[6,6,1,768]{3,2,1,0:T(1,128)S(1)} %get-tuple-element.113), channel_id=1, source_target_pairs={{0,1},{1,2},{2,3},{3,0},{4,5},{5,6},{6,7},{7,4},{8,9},{9,10},{10,1... | collective-permute-start | bytes 331784 | tf_op jit(solution)/shard_map/ppermute | solution.py:21
  52.6 2.1 collective-permute-done.2
  54.7 2.1 collective-permute-done.3
  61.7 4.2 %collective-permute-start.5 = (f32[6,1,32,768]{3,2,1,0:T(8,128)S(1)}, f32[6,1,32,768]{3,2,1,0:T(8,128)S(1)}, u32[]{:S(2)}, u32[]{:S(2)}) collective-permute-start(f32[6,1,32,768]{3,2,1,0:T(8,128)S(1)} %get-tuple-element.120), channel_id=1, source_target_pairs={{4,0},{8,4},{12,8},{16,12},{20,16},{24,20},{28,24},{0,28},{5,1},{9... | collective-permute-start | bytes 1769480 | tf_op jit(solution)/shard_map/ppermute | solution.py:23
  65.9 21.2 %collective-permute-done.4 = f32[6,1,32,768]{3,2,1,0:T(8,128)S(1)} collective-permute-done((f32[6,1,32,768]{3,2,1,0:T(8,128)S(1)}, f32[6,1,32,768]{3,2,1,0:T(8,128)S(1)}, u32[]{:S(2)}, u32[]{:S(2)}) %collective-permute-start.4) | collective-permute-done | bytes 589856 | tf_op jit(solution)/shard_map/ppermute | solution.py:21
  87.1 2.6 %collective-permute-done.5 = f32[6,1,32,768]{3,2,1,0:T(8,128)S(1)} collective-permute-done((f32[6,1,32,768]{3,2,1,0:T(8,128)S(1)}, f32[6,1,32,768]{3,2,1,0:T(8,128)S(1)}, u32[]{:S(2)}, u32[]{:S(2)}) %collective-permute-start.5) | collective-permute-done | bytes 589856 | tf_op jit(solution)/shard_map/ppermute | solution.py:23
  91.5 2.3 collective-permute-done.6
  96.7 2.9 %fusion.44 = (f32[6,4,32,767]{3,2,1,0:T(8,128)S(1)}, f32[6,4,32,767]{3,2,1,0:T(8,128)}) fusion(f32[6,6,34,768]{3,2,1,0:T(8,128)S(1)} %maximum_select_fusion.1), kind=kLoop, calls=%fused_computation.179 | loop fusion | bytes 9424896 | tf_op jit(solution)/shard_map/slice | solution.py:38
  99.6 3.1 %fusion = f32[6,4,32,768]{3,2,1,0:T(8,128)S(1)} fusion(f32[6,6,34,768]{3,2,1,0:T(8,128)S(1)} %maximum_select_fusion.1, f32[6,4,32,767]{3,2,1,0:T(8,128)} %get-tuple-element.108, f32[6,4,32,767]{3,2,1,0:T(8,128)S(1)} %get-tuple-element.107), kind=kLoop, calls=%fused_computation.4 | loop fusion | flops 4128768 | bytes 18868224 | tf_op jit(solution)/shard_map/sub | solution.py:34
  110.4 2.1 copy-done.2
  113.8 4.2 %collective-permute-start.9 = (f32[6,1,34,768]{3,2,1,0:T(8,128)}, f32[6,1,34,768]{3,2,1,0:T(8,128)}, u32[]{:S(2)}, u32[]{:S(2)}) collective-permute-start(f32[6,1,34,768]{3,2,1,0:T(8,128)} %get-tuple-element.104), channel_id=1, source_target_pairs={{4,0},{8,4},{12,8},{16,12},{20,16},{24,20},{28,24},{0,28},{5,1},{9... | collective-permute-start | bytes 1880072 | tf_op jit(solution)/shard_map/ppermute | solution.py:23
  117.9 2.2 slice.467
  120.2 25.3 %collective-permute-done.8 = f32[6,1,34,768]{3,2,1,0:T(8,128)} collective-permute-done((f32[6,1,34,768]{3,2,1,0:T(8,128)}, f32[6,1,34,768]{3,2,1,0:T(8,128)}, u32[]{:S(2)}, u32[]{:S(2)}) %collective-permute-start.8) | collective-permute-done | bytes 626720 | tf_op jit(solution)/shard_map/ppermute | solution.py:21
  145.5 3.1 %collective-permute-done.9 = f32[6,1,34,768]{3,2,1,0:T(8,128)} collective-permute-done((f32[6,1,34,768]{3,2,1,0:T(8,128)}, f32[6,1,34,768]{3,2,1,0:T(8,128)}, u32[]{:S(2)}, u32[]{:S(2)}) %collective-permute-start.9) | collective-permute-done | bytes 626720 | tf_op jit(solution)/shard_map/ppermute | solution.py:23
  157.0 2.1 scatter-add.16
  163.9 2.2 fusion.16
  166.8 4.0 %multiply_reduce_fusion = (f32[]{:T(128)}, f32[6,4,32,768]{3,2,1,0:T(8,128)}) fusion(f32[6,4,32,768]{3,2,1,0:T(8,128)S(1)} %copy-done.4, f32[1,4,32,768]{3,2,1,0:T(8,128)S(1)} %get-tuple-element.106, f32[4,4,32,768]{3,2,1,0:T(8,128)} %get-tuple-element.97, f32[1,4,32,768]{3,2,1,0:T(8,128)S(1)} %get-tuple-element.94), kind=kLoop, calls=%fused_computation.18 | loop fusion | flops 2359295 | bytes 7077892 | tf_op jit(solution)/shard_map/reduce_sum | solution.py:94
  170.8 39.4 %psum.23 = f32[]{:T(128)} all-reduce(f32[]{:T(128)} %get-tuple-element.90), channel_id=1, replica_groups=mesh['gz'=8,'gy'=4] {'gz','gy'}, use_global_device_ids=true, to_apply=%region_8.9 | all-reduce | flops 1 | bytes 8 | tf_op jit(solution)/shard_map/psum | solution.py:94
  210.2 23.4 %all-reduce.20.cloned.1.call-done = f32[32,768]{1,0:T(8,128)} async-done(((f32[32,768]{1,0:T(8,128)}), f32[32,768]{1,0:T(8,128)}) %all-reduce.20.cloned.1.call-update) | async-done | bytes 98320 | tf_op jit(solution)/shard_map/psum | solution.py:77
  (68 shorter events, 40.6 us)
Async XLA Ops:
  7.2 226.4 %all-reduce.20.cloned.1.call-start = ((), (), s32[]{:S(2)}) async-start(), calls=%async_computation | async-start | bytes 196608 | tf_op jit(solution)/shard_map/psum | solution.py:77
  14.1 5.4 %copy-start.6 = (f32[4,32,768]{2,1,0:T(8,128)S(1)}, f32[4,32,768]{2,1,0:T(8,128)}, u32[]{:S(2)}) copy-start(f32[4,32,768]{2,1,0:T(8,128)} %param.15) | copy-start | bytes 1179652
  14.1 5.4 %copy-start.7 = (f32[4,32,768]{2,1,0:T(8,128)S(1)}, f32[4,32,768]{2,1,0:T(8,128)}, u32[]{:S(2)}) copy-start(f32[4,32,768]{2,1,0:T(8,128)} %param.14) | copy-start | bytes 1179652
  20.6 27.0 %collective-permute-start = (f32[6,1,32,768]{3,2,1,0:T(8,128)}, f32[6,1,32,768]{3,2,1,0:T(8,128)S(1)}, u32[]{:S(2)}, u32[]{:S(2)}) collective-permute-start(f32[6,1,32,768]{3,2,1,0:T(8,128)} %get-tuple-element.121), channel_id=1, source_target_pairs={{0,4},{4,8},{8,12},{12,16},{16,20},{20,24},{24,28},{28,0},{1,5},{5... | collective-permute-start | bytes 1769480 | tf_op jit(solution)/shard_map/ppermute | solution.py:21
  22.7 26.7 %collective-permute-start.1 = (f32[6,1,32,768]{3,2,1,0:T(8,128)}, f32[6,1,32,768]{3,2,1,0:T(8,128)S(1)}, u32[]{:S(2)}, u32[]{:S(2)}) collective-permute-start(f32[6,1,32,768]{3,2,1,0:T(8,128)} %get-tuple-element.122), channel_id=1, source_target_pairs={{4,0},{8,4},{12,8},{16,12},{20,16},{24,20},{28,24},{0,28},{5,1},{9... | collective-permute-start | bytes 1769480 | tf_op jit(solution)/shard_map/ppermute | solution.py:23
  49.6 5.1 %collective-permute-start.2 = (f32[6,6,1,768]{3,2,1,0:T(1,128)S(1)}, f32[6,6,1,768]{3,2,1,0:T(1,128)S(1)}, u32[]{:S(2)}, u32[]{:S(2)}) collective-permute-start(f32[6,6,1,768]{3,2,1,0:T(1,128)S(1)} %get-tuple-element.113), channel_id=1, source_target_pairs={{0,1},{1,2},{2,3},{3,0},{4,5},{5,6},{6,7},{7,4},{8,9},{9,10},{10,1... | collective-permute-start | bytes 331784 | tf_op jit(solution)/shard_map/ppermute | solution.py:21
  52.6 4.2 %collective-permute-start.3 = (f32[6,6,1,768]{3,2,1,0:T(1,128)S(1)}, f32[6,6,1,768]{3,2,1,0:T(1,128)S(1)}, u32[]{:S(2)}, u32[]{:S(2)}) collective-permute-start(f32[6,6,1,768]{3,2,1,0:T(1,128)S(1)} %get-tuple-element.114), channel_id=1, source_target_pairs={{1,0},{2,1},{3,2},{0,3},{5,4},{6,5},{7,6},{4,7},{9,8},{10,9},{11,1... | collective-permute-start | bytes 331784 | tf_op jit(solution)/shard_map/ppermute | solution.py:23
  57.8 2.9 %copy-start.1 = (f32[6,6,34,768]{3,2,1,0:T(8,128)}, f32[6,6,34,768]{3,2,1,0:T(8,128)S(1)}, u32[]{:S(2)}) copy-start(f32[6,6,34,768]{3,2,1,0:T(8,128)S(1)} %maximum_select_fusion) | copy-start | bytes 11280388
  60.3 0.9 copy-start.8
  61.7 25.4 %collective-permute-start.4 = (f32[6,1,32,768]{3,2,1,0:T(8,128)S(1)}, f32[6,1,32,768]{3,2,1,0:T(8,128)S(1)}, u32[]{:S(2)}, u32[]{:S(2)}) collective-permute-start(f32[6,1,32,768]{3,2,1,0:T(8,128)S(1)} %get-tuple-element.119), channel_id=1, source_target_pairs={{0,4},{4,8},{8,12},{12,16},{16,20},{20,24},{24,28},{28,0},{1,5},{5... | collective-permute-start | bytes 1769480 | tf_op jit(solution)/shard_map/ppermute | solution.py:21
  61.7 27.9 %collective-permute-start.5 = (f32[6,1,32,768]{3,2,1,0:T(8,128)S(1)}, f32[6,1,32,768]{3,2,1,0:T(8,128)S(1)}, u32[]{:S(2)}, u32[]{:S(2)}) collective-permute-start(f32[6,1,32,768]{3,2,1,0:T(8,128)S(1)} %get-tuple-element.120), channel_id=1, source_target_pairs={{4,0},{8,4},{12,8},{16,12},{20,16},{24,20},{28,24},{0,28},{5,1},{9... | collective-permute-start | bytes 1769480 | tf_op jit(solution)/shard_map/ppermute | solution.py:23
  89.8 4.0 %collective-permute-start.6 = (f32[6,6,1,768]{3,2,1,0:T(1,128)S(1)}, f32[6,6,1,768]{3,2,1,0:T(1,128)S(1)}, u32[]{:S(2)}, u32[]{:S(2)}) collective-permute-start(f32[6,6,1,768]{3,2,1,0:T(1,128)S(1)} %get-tuple-element.111), channel_id=1, source_target_pairs={{0,1},{1,2},{2,3},{3,0},{4,5},{5,6},{6,7},{7,4},{8,9},{9,10},{10,1... | collective-permute-start | bytes 331784 | tf_op jit(solution)/shard_map/ppermute | solution.py:21
  91.5 4.2 %collective-permute-start.7 = (f32[6,6,1,768]{3,2,1,0:T(1,128)S(1)}, f32[6,6,1,768]{3,2,1,0:T(1,128)S(1)}, u32[]{:S(2)}, u32[]{:S(2)}) collective-permute-start(f32[6,6,1,768]{3,2,1,0:T(1,128)S(1)} %get-tuple-element.112), channel_id=1, source_target_pairs={{1,0},{2,1},{3,2},{0,3},{5,4},{6,5},{7,6},{4,7},{9,8},{10,9},{11,1... | collective-permute-start | bytes 331784 | tf_op jit(solution)/shard_map/ppermute | solution.py:23
  96.7 9.3 %copy-start = (f32[6,6,34,768]{3,2,1,0:T(8,128)}, f32[6,6,34,768]{3,2,1,0:T(8,128)S(1)}, u32[]{:S(2)}) copy-start(f32[6,6,34,768]{3,2,1,0:T(8,128)S(1)} %maximum_select_fusion.1) | copy-start | bytes 11280388
  99.6 3.1 %copy-start.4 = (f32[6,4,32,768]{3,2,1,0:T(8,128)S(1)}, f32[6,4,32,768]{3,2,1,0:T(8,128)}, u32[]{:S(2)}) copy-start(f32[6,4,32,768]{3,2,1,0:T(8,128)} %param.19) | copy-start | bytes 7077892
  104.5 0.9 copy-start.9
  110.4 2.1 copy-start.2
  113.8 31.7 %collective-permute-start.8 = (f32[6,1,34,768]{3,2,1,0:T(8,128)}, f32[6,1,34,768]{3,2,1,0:T(8,128)}, u32[]{:S(2)}, u32[]{:S(2)}) collective-permute-start(f32[6,1,34,768]{3,2,1,0:T(8,128)} %get-tuple-element.105), channel_id=1, source_target_pairs={{0,4},{4,8},{8,12},{12,16},{16,20},{20,24},{24,28},{28,0},{1,5},{5... | collective-permute-start | bytes 1880072 | tf_op jit(solution)/shard_map/ppermute | solution.py:21
  113.8 34.8 %collective-permute-start.9 = (f32[6,1,34,768]{3,2,1,0:T(8,128)}, f32[6,1,34,768]{3,2,1,0:T(8,128)}, u32[]{:S(2)}, u32[]{:S(2)}) collective-permute-start(f32[6,1,34,768]{3,2,1,0:T(8,128)} %get-tuple-element.104), channel_id=1, source_target_pairs={{4,0},{8,4},{12,8},{16,12},{20,16},{24,20},{28,24},{0,28},{5,1},{9... | collective-permute-start | bytes 1880072 | tf_op jit(solution)/shard_map/ppermute | solution.py:23
  117.9 30.6 %copy-start.3 = (f32[6,6,34,768]{3,2,1,0:T(8,128)S(1)}, f32[6,6,34,768]{3,2,1,0:T(8,128)}, u32[]{:S(2)}) copy-start(f32[6,6,34,768]{3,2,1,0:T(8,128)} %copy-done.2) | copy-start | bytes 11280388
  149.9 4.9 %collective-permute-start.10 = (f32[6,8,1,768]{3,1,2,0:T(8,128)S(1)}, f32[6,8,1,768]{3,1,2,0:T(8,128)S(1)}, u32[]{:S(2)}, u32[]{:S(2)}) collective-permute-start(f32[6,8,1,768]{3,1,2,0:T(8,128)S(1)} %copy.48), channel_id=1, source_target_pairs={{0,1},{1,2},{2,3},{3,0},{4,5},{5,6},{6,7},{7,4},{8,9},{9,10},{10,1... | collective-permute-start | bytes 442376 | tf_op jit(solution)/shard_map/ppermute | solution.py:21
  152.3 6.8 %collective-permute-start.11 = (f32[6,8,1,768]{3,1,2,0:T(8,128)}, f32[6,8,1,768]{3,1,2,0:T(8,128)}, u32[]{:S(2)}, u32[]{:S(2)}) collective-permute-start(f32[6,8,1,768]{3,1,2,0:T(8,128)} %copy.50), channel_id=1, source_target_pairs={{1,0},{2,1},{3,2},{0,3},{5,4},{6,5},{7,6},{4,7},{9,8},{10,9},{11,1... | collective-permute-start | bytes 442376 | tf_op jit(solution)/shard_map/ppermute | solution.py:23
  154.9 1.4 copy-start.5
Sparse Core Ops, SparseCore 0:
  166.9 66.5 all-reduce.19
where the time goes:
time: 245 us; the launch traced here: 242 us
  waiting for transfers between devices  108 us (44%)
  blocking collectives  39.4 us (16%)
  other arithmetic  37.4 us (15%)
  local copies, waits for them, and re-layouts  23.4 us (10%)
  starting transfers between devices  19.9 us (8%)
  between operations  14.3 us (6%)
    ppermute x6, waiting for transfers between devices, padded_2(): lax.ppermute(tail, axis, [(i, (i + 1) % count) for i in range(count)])  72.7 us
    psum x1, blocking collectives, on_device(): objective = lax.psum(jnp.sum(cotangent * fields_now), ('gz', 'gy'))  39.4 us
    psum x1, waiting for transfers between devices, cycle_total(): return lax.psum(partial_value, 'gz')  23.4 us
    ppermute x6, waiting for transfers between devices, padded_2(): lax.ppermute(head, axis, [((i + 1) % count, i) for i in range(count)])  11.4 us
    ppermute x6, starting transfers between devices, padded_2(): lax.ppermute(head, axis, [((i + 1) % count, i) for i in range(count)])  11.4 us
    ppermute x6, starting transfers between devices, padded_2(): lax.ppermute(tail, axis, [(i, (i + 1) % count) for i in range(count)])  8.5 us
    unnamed x21, local copies, waits for them, and re-layouts  5.95 us
    add x1, other arithmetic, expand_labels(): total + jnp.where(grain_ids[None] == grain, quat_table[grain][:, None, No...  5.4 us
  transfers between devices with their start and end apart: 13, of which 11 were waited for; matrix products, arithmetic and copies ran while one was open for 5% of the time, Pallas kernels for 0%

commit v1 on v0

v1 whole, which is shorter than its diff:
```python
import functools

import jax
import jax.numpy as jnp
from jax import lax
from jax.experimental import pallas as pl
from jax.experimental.pallas import tpu as pltpu
from jax.sharding import PartitionSpec as P

MESH = pl.DeviceIdType.MESH
F32 = jnp.float32


def kernel(
    n, m, depth, rows, cols, per,
    phase, solute, labels, table, heat, cot,
    out, sens_out, obj_out,
    E, lab, M, G, GP, CQ, W0, sbuf, rbuf, obuf, orbuf, red, fin,
    lsem, ysend, yrecv, zsend, zrecv, csend, crecv, r1s, r1r, os, orr, r2s, r2r,
):
    gz = lax.axis_index("gz")
    gy = lax.axis_index("gy")
    up = lax.rem(gz + 1, n)
    down = lax.rem(gz + n - 1, n)
    is_low = gy == 0
    is_high = gy == m - 1
    low = jnp.maximum(gy - 1, 0)
    high = jnp.minimum(gy + 1, m - 1)
    tiles = rows // 8
    lanes = cols // 128
    D = depth
    own = pl.ds(8, rows)
    top = 8 + rows

    bar = pltpu.get_barrier_semaphore()
    for d in range(1, n):
        pl.semaphore_signal(bar, inc=1, device_id=(lax.rem(gz + d, n), gy), device_id_type=MESH)
    for d in range(1, m):
        pl.semaphore_signal(bar, inc=1, device_id=(gz, lax.rem(gy + d, m)), device_id_type=MESH)

    local = []
    dests = ((phase, E.at[0]), (solute, E.at[5]), (labels, lab))
    for k, (src, dst) in enumerate(dests):
        local.append(pltpu.make_async_copy(src, dst.at[pl.ds(2, D), own], lsem.at[k]))
    local.append(pltpu.make_async_copy(cot.at[0], G.at[0, pl.ds(1, D), own], lsem.at[3]))
    local.append(pltpu.make_async_copy(cot.at[5], G.at[1, pl.ds(1, D), own], lsem.at[4]))
    local.append(pltpu.make_async_copy(cot.at[pl.ds(1, 4)], CQ, lsem.at[5]))
    for copy in local:
        copy.start()

    pl.semaphore_wait(bar, n - 1 + m - 1)

    def remote(src, dst, ss, rs, z, y):
        return pltpu.make_async_remote_copy(
            src_ref=src, dst_ref=dst, send_sem=ss, recv_sem=rs, device_id=(z, y), device_id_type=MESH
        )

    zc = {1: [], 2: []}
    i = 0
    for width in (1, 2):
        for src, dst in dests:
            zc[width].append(remote(src.at[D - width], dst.at[2 - width, own], zsend.at[i], zrecv.at[i], up, gy))
            zc[width].append(
                remote(src.at[width - 1], dst.at[D + 1 + width, own], zsend.at[i + 1], zrecv.at[i + 1], down, gy)
            )
            i += 2
    for copy in zc[1]:
        copy.start()
    to_high, to_low = [], []
    faces = [(s, d.at[pl.ds(2, D)]) for s, d in dests]
    faces += [(cot.at[0], G.at[0, pl.ds(1, D)]), (cot.at[5], G.at[1, pl.ds(1, D)])]
    for k, (src, dst) in enumerate(faces):
        to_high.append(
            remote(src.at[:, pl.ds(rows - 8, 8)], dst.at[:, pl.ds(0, 8)], ysend.at[k], yrecv.at[k], gz, high)
        )
        to_low.append(
            remote(src.at[:, pl.ds(0, 8)], dst.at[:, pl.ds(top, 8)], ysend.at[5 + k], yrecv.at[5 + k], gz, low)
        )

    @pl.when(jnp.logical_not(is_high))
    def _():
        for copy in to_high:
            copy.start()

    @pl.when(jnp.logical_not(is_low))
    def _():
        for copy in to_low:
            copy.start()

    for copy in zc[2]:
        copy.start()

    row = lax.broadcasted_iota(jnp.int32, (8, 128), 0)
    lane = lax.broadcasted_iota(jnp.int32, (8, 128), 1)
    zero = jnp.zeros((8, 128), F32)

    sbuf[...] = jnp.zeros_like(sbuf)
    obuf[...] = jnp.zeros_like(obuf)
    for z in (0, D + 1):
        G[1, z] = jnp.zeros((rows + 16, cols), F32)
        GP[z] = jnp.zeros((rows + 16, cols), F32)

    def ds8(t):
        return pl.ds(pl.multiple_of(t * 8, 8), 8)

    def expand(z, t):
        r = ds8(t)
        for j in range(lanes):
            x = pl.ds(j * 128, 128)
            ids = lab[z, r, x]
            for k in range(4):
                E[1 + k, z, r, x] = jnp.take_along_axis(table[k], ids, axis=1)

    def wipe(z, t):
        r = ds8(t)
        for k in range(6):
            E[k, z, r, :] = jnp.zeros((8, cols), F32)

    def loop(count, body):
        def step(i, carry):
            body(i)
            return carry

        lax.fori_loop(0, count, step, 0)

    def around(ref, lead, z, t, j, last):
        r, x = ds8(t), pl.ds(j * 128, 128)
        c = ref[(*lead, z, r, x)]
        before = ref[(*lead, z, ds8(jnp.maximum(t - 1, 0)), x)]
        after = ref[(*lead, z, ds8(jnp.minimum(t + 1, last)), x)]
        left = ref[(*lead, z, r, pl.ds((j - 1) * 128, 128))] if j else zero
        right = ref[(*lead, z, r, pl.ds((j + 1) * 128, 128))] if j < lanes - 1 else zero
        ys = pltpu.roll(jnp.where(row == 0, after, c), 7, 0) + pltpu.roll(jnp.where(row == 7, before, c), 1, 0)
        xs = pltpu.roll(jnp.where(lane == 0, right, c), 127, 1) + pltpu.roll(jnp.where(lane == 127, left, c), 1, 1)
        zs = ref[(*lead, z + 1, r, x)] + ref[(*lead, z - 1, r, x)]
        return c, zs + ys + xs - 6.0 * c

    def mid(z, t, inside):
        r = ds8(t)
        drop = ((t == 0) & is_low) | ((t == tiles + 1) & is_high)
        keep = jnp.where(drop, 0.0, 1.0)
        hr = ds8(t)
        for j in range(lanes):
            x = pl.ds(j * 128, 128)
            p, lp = around(E, (0,), z, t, j, tiles + 1)
            c, lc = around(E, (5,), z, t, j, tiles + 1)
            misfit = zero
            rate = 0.08 * ((1.0 - p) * (1.0 - p) + 0.1)
            for k in range(4):
                q, lq = around(E, (1 + k,), z, t, j, tiles + 1)
                misfit = misfit + q * lq
                M[1 + k, z - 1, r, x] = keep * (q + rate * lq)
            th = jnp.tanh(heat[hr, x] - 0.5 * c)
            pq = p * (1.0 - p)
            dp = 0.08 * (lp + 4.0 * pq * (p - 0.5 + 0.6 * th) + 0.2 * p * misfit)
            cn = keep * (c + 0.064 * lc + 0.5 * dp * c)
            M[0, z - 1, r, x] = keep * (p + dp)
            M[5, z - 1, r, x] = cn
            W0[z - 1, r, x] = 0.192 * pq * (1.0 - th * th)
            if inside:
                GP[z - 1, r, x] = G[0, z - 1, r, x] + 0.5 * cn * G[1, z - 1, r, x]

    def final(z, t, edge):
        zm = z - 1
        r = ds8(t)
        ro = ds8(t - 1)
        for j in range(lanes):
            x = pl.ds(j * 128, 128)
            p, lp = around(M, (0,), zm, t, j, tiles + 1)
            c, lc = around(M, (5,), zm, t, j, tiles + 1)
            gc, lgc = around(G, (1,), zm, t, j, tiles + 1)
            gp, lgp = around(GP, (), zm, t, j, tiles + 1)
            g0 = G[0, zm, r, x]
            rate = 0.08 * ((1.0 - p) * (1.0 - p) + 0.1)
            misfit, qterm, obj = zero, zero, zero
            for k in range(4):
                q, lq = around(M, (1 + k,), zm, t, j, tiles + 1)
                g = CQ[k, z - 2, ro, x]
                qn = q + rate * lq
                out[1 + k, z - 2, ro, x] = qn
                misfit = misfit + q * lq
                qterm = qterm + g * lq
                obj = obj + g * qn
            th = jnp.tanh(heat[r, x] - 0.5 * c)
            pq = p * (1.0 - p)
            drive = p - 0.5 + 0.6 * th
            dp = 0.08 * (lp + 4.0 * pq * drive + 0.2 * p * misfit)
            pn = p + dp
            cn = c + 0.064 * lc + 0.5 * dp * c
            out[0, z - 2, ro, x] = pn
            out[5, z - 2, ro, x] = cn
            obuf[...] += obj + g0 * pn + gc * cn
            w = 0.192 * pq * (1.0 - th * th)
            gw = gp * w
            lam_p = (
                gp * (1.0 + 0.08 * (4.0 * (1.0 - 2.0 * p) * drive + 4.0 * pq + 0.2 * misfit))
                + 0.08 * lgp
                - 0.5 * c * gc
                - 0.16 * (1.0 - p) * qterm
            )
            lam_c = gc * (1.0 + 0.5 * dp) + 0.064 * lgc - 0.5 * gw
            s = gw + (lam_p + 0.5 * E[5, z, r, x] * lam_c) * W0[zm, r, x]
            if edge is not None:
                s = s + W0[edge - 1, r, x] * (0.08 * gp + 0.032 * E[5, edge, r, x] * gc)
            b = (t - 1) * lanes + j
            sbuf[b] += s

    def grid(z0, zstep, t0, count, body):
        loop(2 * count, lambda i: body(z0 + zstep * (i // count), t0 + i % count))

    for copy in local[:3]:
        copy.wait()
    loop(D * tiles, lambda i: expand(2 + i // tiles, 1 + i % tiles))

    @pl.when(jnp.logical_not(is_low))
    def _():
        for copy in to_high:
            copy.wait_recv()
        loop(D, lambda i: expand(2 + i, 0))

    @pl.when(is_low)
    def _():
        loop(D + 2, lambda i: wipe(1 + i, 0))
        for k in range(2):
            for z in range(D):
                G[k, 1 + z, pl.ds(0, 8), :] = jnp.zeros((8, cols), F32)

    @pl.when(jnp.logical_not(is_high))
    def _():
        for copy in to_low:
            copy.wait_recv()
        loop(D, lambda i: expand(2 + i, tiles + 1))

    @pl.when(is_high)
    def _():
        loop(D + 2, lambda i: wipe(1 + i, tiles + 1))
        for k in range(2):
            for z in range(D):
                G[k, 1 + z, pl.ds(top, 8), :] = jnp.zeros((8, cols), F32)

    for copy in local[3:]:
        copy.wait()
    loop((D - 2) * (tiles + 2), lambda i: mid(3 + i // (tiles + 2), i % (tiles + 2), True))

    for copy in zc[1]:
        copy.wait_recv()
    c_high, c_low = [], []
    i = 0
    for z in (1, D + 2):
        for _, dst in dests:
            c_high.append(
                remote(dst.at[z, pl.ds(rows, 8)], dst.at[z, pl.ds(0, 8)], csend.at[i], crecv.at[i], gz, high)
            )
            c_low.append(
                remote(dst.at[z, pl.ds(8, 8)], dst.at[z, pl.ds(top, 8)], csend.at[6 + i], crecv.at[6 + i], gz, low)
            )
            i += 1

    @pl.when(jnp.logical_not(is_high))
    def _():
        for copy in c_high:
            copy.start()

    @pl.when(jnp.logical_not(is_low))
    def _():
        for copy in c_low:
            copy.start()

    grid(1, D + 1, 1, tiles, expand)

    @pl.when(jnp.logical_not(is_low))
    def _():
        for copy in c_high:
            copy.wait_recv()
        loop(2, lambda i: expand(1 + (D + 1) * i, 0))

    @pl.when(jnp.logical_not(is_high))
    def _():
        for copy in c_low:
            copy.wait_recv()
        loop(2, lambda i: expand(1 + (D + 1) * i, tiles + 1))

    grid(2, D - 1, 0, tiles + 2, lambda z, t: mid(z, t, True))
    loop((D - 2) * tiles, lambda i: final(3 + i // tiles, 1 + i % tiles, None))

    for copy in zc[2]:
        copy.wait_recv()
    grid(0, D + 3, 1, tiles, expand)
    grid(1, D + 1, 1, tiles, lambda z, t: mid(z, t, False))
    loop(2 * tiles, lambda i: final(2 + (D - 1) * (i // tiles), 1 + i % tiles, 1 + (D + 1) * (i // tiles)))

    sends = []
    for d in range(1, n):
        peer = lax.rem(gz + d, n)
        sends.append(remote(sbuf.at[pl.ds(peer * per, per)], rbuf.at[d - 1], r1s.at[d - 1], r1r.at[d - 1], peer, gy))
    for d in range(1, m):
        sends.append(remote(obuf, orbuf.at[gy], os.at[d - 1], orr.at[d - 1], gz, lax.rem(gy + d, m)))
    for copy in sends:
        copy.start()
    orbuf[gy] = obuf[...]
    for copy in sends:
        copy.wait_recv()
    acc = sbuf[pl.ds(gz * per, per)]
    for d in range(1, n):
        acc = acc + rbuf[d - 1]
    red[pl.ds(0, per)] = acc
    total = orbuf[0]
    for d in range(1, m):
        total = total + orbuf[d]
    red[per] = total
    bcast = []
    for d in range(1, n):
        bcast.append(remote(red, fin.at[gz], r2s.at[d - 1], r2r.at[d - 1], lax.rem(gz + d, n), gy))
    for copy in bcast:
        copy.start()
    fin[gz] = red[...]
    for copy in bcast:
        copy.wait_recv()
    total = fin[0, per]
    for d in range(1, n):
        total = total + fin[d, per]
    obj_out[0, 0] = jnp.sum(total)
    for b in range(tiles * lanes):
        sens_out[pl.ds(b // lanes * 8, 8), pl.ds(b % lanes * 128, 128)] = fin[b // per, b % per]

    for copy in zc[1] + zc[2] + sends + bcast:
        copy.wait_send()

    @pl.when(jnp.logical_not(is_high))
    def _():
        for copy in to_high + c_high:
            copy.wait_send()

    @pl.when(jnp.logical_not(is_low))
    def _():
        for copy in to_low + c_low:
            copy.wait_send()


def solution(mesh):
    n, m = mesh.shape["gz"], mesh.shape["gy"]

    def on_device(phase, solute, labels, quat_table, heat_map, cotangent):
        depth, rows, cols = phase.shape
        grains = quat_table.shape[0]
        blocks = rows // 8 * (cols // 128)
        per = -(-blocks // n)
        table = jnp.pad(quat_table.T, ((0, 0), (0, 128 - grains)))
        table = jnp.broadcast_to(table[:, None, :], (4, 8, 128))
        gy = lax.axis_index("gy")
        above = lax.ppermute(heat_map[-8:], "gy", [(i, i + 1) for i in range(m - 1)])
        below = lax.ppermute(heat_map[:8], "gy", [(i + 1, i) for i in range(m - 1)])
        heat = jnp.concatenate([above, heat_map, below], 0)
        tall = rows + 16
        vmem = pl.BlockSpec(memory_space=pltpu.VMEM)
        hbm = pl.BlockSpec(memory_space=pl.ANY)
        dma = lambda k: pltpu.SemaphoreType.DMA((k,))
        final, sens, obj = pl.pallas_call(
            functools.partial(kernel, n, m, depth, rows, cols, per),
            out_shape=(
                jax.ShapeDtypeStruct((6, depth, rows, cols), F32),
                jax.ShapeDtypeStruct((rows, cols), F32),
                jax.ShapeDtypeStruct((1, 1), F32),
            ),
            in_specs=[hbm, hbm, hbm, vmem, vmem, hbm],
            out_specs=(vmem, vmem, pl.BlockSpec(memory_space=pltpu.SMEM)),
            scratch_shapes=[
                pltpu.VMEM((6, depth + 4, tall, cols), F32),
                pltpu.VMEM((depth + 4, tall, cols), jnp.int32),
                pltpu.VMEM((6, depth + 2, tall, cols), F32),
                pltpu.VMEM((2, depth + 2, tall, cols), F32),
                pltpu.VMEM((depth + 2, tall, cols), F32),
                pltpu.VMEM((4, depth, rows, cols), F32),
                pltpu.VMEM((depth + 2, tall, cols), F32),
                pltpu.VMEM((n * per, 8, 128), F32),
                pltpu.VMEM((n - 1, per, 8, 128), F32),
                pltpu.VMEM((8, 128), F32),
                pltpu.VMEM((m, 8, 128), F32),
                pltpu.VMEM((per + 1, 8, 128), F32),
                pltpu.VMEM((n, per + 1, 8, 128), F32),
                dma(6), dma(10), dma(10), dma(12), dma(12), dma(12), dma(12),
                dma(n - 1), dma(n - 1), dma(m - 1), dma(m - 1), dma(n - 1), dma(n - 1),
            ],
            compiler_params=pltpu.CompilerParams(
                collective_id=0, has_side_effects=True, vmem_limit_bytes=48 * 1024 * 1024
            ),
        )(phase, solute, labels, table, heat, cotangent)
        return final, sens, obj[0, 0]

    return jax.shard_map(
        on_device,
        mesh=mesh,
        in_specs=(
            P("gz", "gy", None),
            P("gz", "gy", None),
            P("gz", "gy", None),
            P(),
            P("gy", None),
            P(None, "gz", "gy", None),
        ),
        out_specs=(P(None, "gz", "gy", None), P("gy", None), P()),
        check_vma=False,
    )
```

time: 245 us -> 66 us (0.27)
  waiting for transfers between devices: 108 us -> 2.53 us
  Pallas kernels: 0 us -> 45 us
  blocking collectives: 39.4 us -> 0 us
  other arithmetic: 37.4 us -> 0.9 us
  local copies, waits for them, and re-layouts: 23.4 us -> 8.15 us
  starting transfers between devices: 19.9 us -> 6.42 us
  between operations: 14.3 us -> 2.37 us
    ppermute x12 -> x2, waiting for transfers between devices: 84.2 us -> 2.53 us  [the longest x1 2.52 us: on_device(): below = lax.ppermute(heat_map[:8], 'gy', [(i + 1, i) for i in range(m - 1)])]
    pallas_call x0 -> x1, Pallas kernels: none -> 45 us  [on_device(): pl.pallas_call(functools.partial(kernel, n, m, depth, rows, cols, per), o...]
    psum x1 -> x0, blocking collectives: 39.4 us -> none  [on_device(): objective = lax.psum(jnp.sum(cotangent * fields_now), ('gz', 'gy'))]
    psum x1 -> x0, waiting for transfers between devices: 23.4 us -> none  [cycle_total(): return lax.psum(partial_value, 'gz')]
    ppermute x12 -> x2, starting transfers between devices: 19.9 us -> 6.42 us  [the longest x1 4.5 us: on_device(): lax.ppermute(heat_map[-8:], 'gy', [(i, i + 1) for i in range(m - 1)])]
    slice x10 -> x1, local copies, waits for them, and re-layouts: 12.5 us -> 0.76 us  [on_device(): heat_map[-8:]]
    add x6 -> x0, other arithmetic: 9.3 us -> none  [the longest x1 5.4 us: expand_labels(): total + jnp.where(grain_ids[None] == grain, quat_table[grain][:, None, No...]
    reduce_sum x3 -> x0, other arithmetic: 8.01 us -> none  [the longest x1 3.99 us: on_device(): objective = lax.psum(jnp.sum(cotangent * fields_now), ('gz', 'gy'))]
  transfers between devices with their start and end apart: 13 -> 2, of which waited for: 11 -> 1; matrix products, arithmetic and copies ran while one was open for 5% -> 1% of each run, Pallas kernels for 0% -> 0%
where the time goes in v1:
time: 66 us; the launch traced here: 65.4 us
  Pallas kernels  45 us (68%)
  local copies, waits for them, and re-layouts  8.15 us (12%)
  starting transfers between devices  6.42 us (10%)
  waiting for transfers between devices  2.53 us (4%)
  between operations  2.37 us (4%)
  other arithmetic  0.9 us (1%)
    pallas_call x1, Pallas kernels, on_device(): pl.pallas_call(functools.partial(kernel, n, m, depth, rows, cols, per), o...  45 us
    unnamed x10, local copies, waits for them, and re-layouts  6.69 us
    ppermute x1, starting transfers between devices, on_device(): lax.ppermute(heat_map[-8:], 'gy', [(i, i + 1) for i in range(m - 1)])  4.5 us
    ppermute x1, waiting for transfers between devices, on_device(): below = lax.ppermute(heat_map[:8], 'gy', [(i + 1, i) for i in range(m - 1)])  2.52 us
    ppermute x1, starting transfers between devices, on_device(): below = lax.ppermute(heat_map[:8], 'gy', [(i + 1, i) for i in range(m - 1)])  1.92 us
  transfers between devices with their start and end apart: 2, of which 1 were waited for; matrix products, arithmetic and copies ran while one was open for 1% of the time, Pallas kernels for 0%

profile of v1, /device:TPU:1, one launch (start us, length us, event | category | flops | bytes accessed | tf_op | source)
XLA Modules:
  0.0 65.4 jit_solution(5038970956951518052)
XLA Ops:
  0.6 0.8 %fusion = (f32[8,768]{1,0:T(8,128)S(1)}, f32[8,768]{1,0:T(8,128)S(1)}) fusion(f32[32,768]{1,0:T(8,128)} %param.10), kind=kLoop, calls=%fused_computation.1 | loop fusion | bytes 98304 | tf_op jit(solution)/shard_map/slice | solution.py:351
  1.4 4.5 %collective-permute-start = (f32[8,768]{1,0:T(8,128)S(1)}, f32[8,768]{1,0:T(8,128)S(1)}, u32[]{:S(2)}, u32[]{:S(2)}) collective-permute-start(f32[8,768]{1,0:T(8,128)S(1)} %get-tuple-element.9), channel_id=1, source_target_pairs={{0,1},{1,2},{2,3},{4,5},{5,6},{6,7},{8,9},{9,10},{10,11},{12,13},{... | collective-permute-start | bytes 73736 | tf_op jit(solution)/shard_map/ppermute | solution.py:351
  5.9 1.9 %collective-permute-start.1 = (f32[8,768]{1,0:T(8,128)S(1)}, f32[8,768]{1,0:T(8,128)S(1)}, u32[]{:S(2)}, u32[]{:S(2)}) collective-permute-start(f32[8,768]{1,0:T(8,128)S(1)} %get-tuple-element.10), channel_id=1, source_target_pairs={{1,0},{2,1},{3,2},{5,4},{6,5},{7,6},{9,8},{10,9},{11,10},{13,12},{... | collective-permute-start | bytes 73736 | tf_op jit(solution)/shard_map/ppermute | solution.py:352
  7.8 0.7 %pad.4 = f32[4,128]{1,0:T(4,128)S(1)} pad(f32[4,32]{1,0:T(4,128)} %bitcast.2, f32[]{:T(128)} %constant.2.clone.1), padding=0_0x0_96 | pad | bytes 2564 | tf_op jit(solution)/shard_map/jit(_pad)/pad | solution.py:348
  8.5 0.0 collective-permute-done
  8.5 2.5 %collective-permute-done.1 = f32[8,768]{1,0:T(8,128)S(1)} collective-permute-done((f32[8,768]{1,0:T(8,128)S(1)}, f32[8,768]{1,0:T(8,128)S(1)}, u32[]{:S(2)}, u32[]{:S(2)}) %collective-permute-start.1) | collective-permute-done | bytes 24608 | tf_op jit(solution)/shard_map/ppermute | solution.py:352
  11.0 0.9 %pad_maximum_fusion.heat = f32[48,768]{1,0:T(8,128)S(1)} fusion(f32[8,768]{1,0:T(8,128)S(1)} %collective-permute-done.1, f32[32,768]{1,0:T(8,128)} %param.10, f32[8,768]{1,0:T(8,128)S(1)} %collective-permute-done), kind=kLoop, calls=%fused_computation | loop fusion | flops 73728 | bytes 294912 | tf_op jit(solution)/shard_map/concatenate | solution.py:353
  12.0 0.0 copy-start
  12.0 1.7 %copy-done = f32[6,4,32,768]{3,2,1,0:T(8,128)S(1)} copy-done((f32[6,4,32,768]{3,2,1,0:T(8,128)S(1)}, f32[6,4,32,768]{3,2,1,0:T(8,128)}, u32[]{:S(2)}) %copy-start) | copy-done | bytes 2359320
  13.6 0.0 copy-start.1
  13.6 1.0 %copy-done.1 = f32[4,32,768]{2,1,0:T(8,128)S(1)} copy-done((f32[4,32,768]{2,1,0:T(8,128)S(1)}, f32[4,32,768]{2,1,0:T(8,128)}, u32[]{:S(2)}) %copy-start.1) | copy-done | bytes 393240
  14.6 0.0 copy-start.2
  14.6 1.0 %copy-done.2 = f32[4,32,768]{2,1,0:T(8,128)S(1)} copy-done((f32[4,32,768]{2,1,0:T(8,128)S(1)}, f32[4,32,768]{2,1,0:T(8,128)}, u32[]{:S(2)}) %copy-start.2) | copy-done | bytes 393240
  15.6 0.0 copy-start.3
  15.6 1.0 %copy-done.3 = s32[4,32,768]{2,1,0:T(8,128)S(1)} copy-done((s32[4,32,768]{2,1,0:T(8,128)S(1)}, s32[4,32,768]{2,1,0:T(8,128)}, u32[]{:S(2)}) %copy-start.3) | copy-done | bytes 393240
  16.6 45.0 %shard_map.85 = (f32[6,4,32,768]{3,2,1,0:T(8,128)S(1)}, f32[32,768]{1,0:T(8,128)S(1)}, f32[1,1]{1,0:T(1,128)}) custom-call(f32[4,32,768]{2,1,0:T(8,128)S(1)} %copy-done.1, f32[4,32,768]{2,1,0:T(8,128)S(1)} %copy-done.2, s32[4,32,768]{2,1,0:T(8,128)S(1)} %copy-done.3, f32[4,8,128]{2,1,0:T(8,128)S(1)} %broadcast_in_dim.2.table, ...), custom_call_target="tpu_custom_call" | custom-call | tf_op jit(solution)/shard_map/pallas_call | solution.py:358
  61.6 1.4 %copy.12 = f32[6,4,32,768]{3,2,1,0:T(8,128)} copy(f32[6,4,32,768]{3,2,1,0:T(8,128)S(1)} %get-tuple-element.14) | data formatting | bytes 4718592
  63.0 0.6 copy.13
  (1 shorter events, 0.0 us)
Async XLA Ops:
  1.4 7.1 %collective-permute-start = (f32[8,768]{1,0:T(8,128)S(1)}, f32[8,768]{1,0:T(8,128)S(1)}, u32[]{:S(2)}, u32[]{:S(2)}) collective-permute-start(f32[8,768]{1,0:T(8,128)S(1)} %get-tuple-element.9), channel_id=1, source_target_pairs={{0,1},{1,2},{2,3},{4,5},{5,6},{6,7},{8,9},{9,10},{10,11},{12,13},{... | collective-permute-start | bytes 73736 | tf_op jit(solution)/shard_map/ppermute | solution.py:351
  5.9 5.1 %collective-permute-start.1 = (f32[8,768]{1,0:T(8,128)S(1)}, f32[8,768]{1,0:T(8,128)S(1)}, u32[]{:S(2)}, u32[]{:S(2)}) collective-permute-start(f32[8,768]{1,0:T(8,128)S(1)} %get-tuple-element.10), channel_id=1, source_target_pairs={{1,0},{2,1},{3,2},{5,4},{6,5},{7,6},{9,8},{10,9},{11,10},{13,12},{... | collective-permute-start | bytes 73736 | tf_op jit(solution)/shard_map/ppermute | solution.py:352
  12.0 1.7 %copy-start = (f32[6,4,32,768]{3,2,1,0:T(8,128)S(1)}, f32[6,4,32,768]{3,2,1,0:T(8,128)}, u32[]{:S(2)}) copy-start(f32[6,4,32,768]{3,2,1,0:T(8,128)} %cot.1) | copy-start | bytes 7077892
  13.6 1.0 %copy-start.1 = (f32[4,32,768]{2,1,0:T(8,128)S(1)}, f32[4,32,768]{2,1,0:T(8,128)}, u32[]{:S(2)}) copy-start(f32[4,32,768]{2,1,0:T(8,128)} %phase.1) | copy-start | bytes 1179652
  14.6 1.0 %copy-start.2 = (f32[4,32,768]{2,1,0:T(8,128)S(1)}, f32[4,32,768]{2,1,0:T(8,128)}, u32[]{:S(2)}) copy-start(f32[4,32,768]{2,1,0:T(8,128)} %solute.1) | copy-start | bytes 1179652
  15.6 1.0 %copy-start.3 = (s32[4,32,768]{2,1,0:T(8,128)S(1)}, s32[4,32,768]{2,1,0:T(8,128)}, u32[]{:S(2)}) copy-start(s32[4,32,768]{2,1,0:T(8,128)} %labels.1) | copy-start | bytes 1179652

commit v2 on v1

--- a/solution.py
+++ b/solution.py
@@ -13,10 +13,10 @@
 
 def kernel(
     n, m, depth, rows, cols, per,
-    phase, solute, labels, table, heat, cot,
+    phase, solute, labels, quats, heat_in, cot,
     out, sens_out, obj_out,
-    E, lab, M, G, GP, CQ, W0, sbuf, rbuf, obuf, orbuf, red, fin,
-    lsem, ysend, yrecv, zsend, zrecv, csend, crecv, r1s, r1r, os, orr, r2s, r2r,
+    E, lab, M, G, GP, CQ, W0, heat, table, sbuf, rbuf, obuf, orbuf, red, fin,
+    lsem, ysend, yrecv, zsend, zrecv, fsend, frecv, csend, crecv, r1s, r1r, os, orr, r2s, r2r,
 ):
     gz = lax.axis_index("gz")
     gy = lax.axis_index("gy")
@@ -45,6 +45,7 @@
     local.append(pltpu.make_async_copy(cot.at[0], G.at[0, pl.ds(1, D), own], lsem.at[3]))
     local.append(pltpu.make_async_copy(cot.at[5], G.at[1, pl.ds(1, D), own], lsem.at[4]))
     local.append(pltpu.make_async_copy(cot.at[pl.ds(1, 4)], CQ, lsem.at[5]))
+    local.append(pltpu.make_async_copy(heat_in, heat.at[own], lsem.at[6]))
     for copy in local:
         copy.start()
 
@@ -55,16 +56,22 @@
             src_ref=src, dst_ref=dst, send_sem=ss, recv_sem=rs, device_id=(z, y), device_id_type=MESH
         )
 
-    zc = {1: [], 2: []}
-    i = 0
-    for width in (1, 2):
-        for src, dst in dests:
-            zc[width].append(remote(src.at[D - width], dst.at[2 - width, own], zsend.at[i], zrecv.at[i], up, gy))
-            zc[width].append(
-                remote(src.at[width - 1], dst.at[D + 1 + width, own], zsend.at[i + 1], zrecv.at[i + 1], down, gy)
+    zc = []
+    for k, (src, dst) in enumerate(dests):
+        zc.append(remote(src.at[D - 1], dst.at[1, own], zsend.at[2 * k], zrecv.at[2 * k], up, gy))
+        zc.append(remote(src.at[0], dst.at[D + 2, own], zsend.at[2 * k + 1], zrecv.at[2 * k + 1], down, gy))
+
+    def second(t):
+        found = []
+        a, b = pl.ds(pl.multiple_of(t * 8, 8), 8), pl.ds(pl.multiple_of(t * 8 + 8, 8), 8)
+        for k, (src, dst) in enumerate(dests):
+            found.append(remote(src.at[D - 2, a], dst.at[0, b], fsend.at[2 * k, t], frecv.at[2 * k, t], up, gy))
+            found.append(
+                remote(src.at[1, a], dst.at[D + 3, b], fsend.at[2 * k + 1, t], frecv.at[2 * k + 1, t], down, gy)
             )
-            i += 2
-    for copy in zc[1]:
+        return found
+
+    for copy in zc:
         copy.start()
     to_high, to_low = [], []
     faces = [(s, d.at[pl.ds(2, D)]) for s, d in dests]
@@ -74,8 +81,12 @@
             remote(src.at[:, pl.ds(rows - 8, 8)], dst.at[:, pl.ds(0, 8)], ysend.at[k], yrecv.at[k], gz, high)
         )
         to_low.append(
-            remote(src.at[:, pl.ds(0, 8)], dst.at[:, pl.ds(top, 8)], ysend.at[5 + k], yrecv.at[5 + k], gz, low)
+            remote(src.at[:, pl.ds(0, 8)], dst.at[:, pl.ds(top, 8)], ysend.at[6 + k], yrecv.at[6 + k], gz, low)
         )
+    to_high.append(
+        remote(heat_in.at[pl.ds(rows - 8, 8)], heat.at[pl.ds(0, 8)], ysend.at[5], yrecv.at[5], gz, high)
+    )
+    to_low.append(remote(heat_in.at[pl.ds(0, 8)], heat.at[pl.ds(top, 8)], ysend.at[11], yrecv.at[11], gz, low))
 
     @pl.when(jnp.logical_not(is_high))
     def _():
@@ -87,13 +98,19 @@
         for copy in to_low:
             copy.start()
 
-    for copy in zc[2]:
-        copy.start()
+    for t in range(tiles):
+        for copy in second(t):
+            copy.start()
 
     row = lax.broadcasted_iota(jnp.int32, (8, 128), 0)
     lane = lax.broadcasted_iota(jnp.int32, (8, 128), 1)
     zero = jnp.zeros((8, 128), F32)
 
+    for k in range(4):
+        entry = zero
+        for grain in range(quats.shape[0]):
+            entry = jnp.where(lane == grain, quats[grain, k], entry)
+        table[k] = entry
     sbuf[...] = jnp.zeros_like(sbuf)
     obuf[...] = jnp.zeros_like(obuf)
     for z in (0, D + 1):
@@ -221,6 +238,7 @@
     @pl.when(is_low)
     def _():
         loop(D + 2, lambda i: wipe(1 + i, 0))
+        heat[pl.ds(0, 8), :] = jnp.zeros((8, cols), F32)
         for k in range(2):
             for z in range(D):
                 G[k, 1 + z, pl.ds(0, 8), :] = jnp.zeros((8, cols), F32)
@@ -234,6 +252,7 @@
     @pl.when(is_high)
     def _():
         loop(D + 2, lambda i: wipe(1 + i, tiles + 1))
+        heat[pl.ds(top, 8), :] = jnp.zeros((8, cols), F32)
         for k in range(2):
             for z in range(D):
                 G[k, 1 + z, pl.ds(top, 8), :] = jnp.zeros((8, cols), F32)
@@ -242,7 +261,7 @@
         copy.wait()
     loop((D - 2) * (tiles + 2), lambda i: mid(3 + i // (tiles + 2), i % (tiles + 2), True))
 
-    for copy in zc[1]:
+    for copy in zc:
         copy.wait_recv()
     c_high, c_low = [], []
     i = 0
@@ -283,26 +302,53 @@
     grid(2, D - 1, 0, tiles + 2, lambda z, t: mid(z, t, True))
     loop((D - 2) * tiles, lambda i: final(3 + i // tiles, 1 + i % tiles, None))
 
-    for copy in zc[2]:
-        copy.wait_recv()
-    grid(0, D + 3, 1, tiles, expand)
-    grid(1, D + 1, 1, tiles, lambda z, t: mid(z, t, False))
-    loop(2 * tiles, lambda i: final(2 + (D - 1) * (i // tiles), 1 + i % tiles, 1 + (D + 1) * (i // tiles)))
+    def give(o):
+        return remote(sbuf.at[pl.ds(o * per, per)], rbuf.at[gz], r1s.at[o], r1r.at[gz], o, gy)
+
+    def take(o):
+        return remote(sbuf.at[pl.ds(o * per, per)], rbuf.at[o], r1s.at[o], r1r.at[o], o, gy)
+
+    def others(body):
+        for o in range(n):
+
+            @pl.when(gz != o)
+            def _():
+                body(o)
+
+    given = 0
+    for t in range(tiles):
+        for copy in second(t):
+            copy.wait_recv()
+
+        def layers(i, t=t):
+            z = 1 + (D + 1) * i
+            expand(z - 1 + 2 * i, t + 1)
+            mid(z, t + 1, False)
+            final(2 + (D - 1) * i, t + 1, z)
+
+        loop(2, layers)
+        ready = n if t == tiles - 1 else (t + 1) * lanes // per
+        for o in range(given, ready):
+
+            @pl.when(gz != o)
+            def _():
+                give(o).start()
+
+        given = ready
 
     sends = []
-    for d in range(1, n):
-        peer = lax.rem(gz + d, n)
-        sends.append(remote(sbuf.at[pl.ds(peer * per, per)], rbuf.at[d - 1], r1s.at[d - 1], r1r.at[d - 1], peer, gy))
     for d in range(1, m):
         sends.append(remote(obuf, orbuf.at[gy], os.at[d - 1], orr.at[d - 1], gz, lax.rem(gy + d, m)))
     for copy in sends:
         copy.start()
     orbuf[gy] = obuf[...]
+    rbuf[gz] = jnp.zeros((per, 8, 128), F32)
     for copy in sends:
         copy.wait_recv()
+    others(lambda o: take(o).wait_recv())
     acc = sbuf[pl.ds(gz * per, per)]
-    for d in range(1, n):
-        acc = acc + rbuf[d - 1]
+    for d in range(n):
+        acc = acc + rbuf[d]
     red[pl.ds(0, per)] = acc
     total = orbuf[0]
     for d in range(1, m):
@@ -323,8 +369,12 @@
     for b in range(tiles * lanes):
         sens_out[pl.ds(b // lanes * 8, 8), pl.ds(b % lanes * 128, 128)] = fin[b // per, b % per]
 
-    for copy in zc[1] + zc[2] + sends + bcast:
+    for copy in zc + sends + bcast:
         copy.wait_send()
+    others(lambda o: give(o).wait_send())
+    for t in range(tiles):
+        for copy in second(t):
+            copy.wait_send()
 
     @pl.when(jnp.logical_not(is_high))
     def _():
@@ -342,18 +392,13 @@
 
     def on_device(phase, solute, labels, quat_table, heat_map, cotangent):
         depth, rows, cols = phase.shape
-        grains = quat_table.shape[0]
         blocks = rows // 8 * (cols // 128)
         per = -(-blocks // n)
-        table = jnp.pad(quat_table.T, ((0, 0), (0, 128 - grains)))
-        table = jnp.broadcast_to(table[:, None, :], (4, 8, 128))
-        gy = lax.axis_index("gy")
-        above = lax.ppermute(heat_map[-8:], "gy", [(i, i + 1) for i in range(m - 1)])
-        below = lax.ppermute(heat_map[:8], "gy", [(i + 1, i) for i in range(m - 1)])
-        heat = jnp.concatenate([above, heat_map, below], 0)
         tall = rows + 16
         vmem = pl.BlockSpec(memory_space=pltpu.VMEM)
-        hbm = pl.BlockSpec(memory_space=pl.ANY)
+        hbm = pl.BlockSpec(memory_space=pltpu.HBM)
+        smem = pl.BlockSpec(memory_space=pltpu.SMEM)
+        fine = pltpu.SemaphoreType.DMA((6, rows // 8))
         dma = lambda k: pltpu.SemaphoreType.DMA((k,))
         final, sens, obj = pl.pallas_call(
             functools.partial(kernel, n, m, depth, rows, cols, per),
@@ -362,8 +407,8 @@
                 jax.ShapeDtypeStruct((rows, cols), F32),
                 jax.ShapeDtypeStruct((1, 1), F32),
             ),
-            in_specs=[hbm, hbm, hbm, vmem, vmem, hbm],
-            out_specs=(vmem, vmem, pl.BlockSpec(memory_space=pltpu.SMEM)),
+            in_specs=[hbm, hbm, hbm, smem, hbm, hbm],
+            out_specs=(vmem, vmem, smem),
             scratch_shapes=[
                 pltpu.VMEM((6, depth + 4, tall, cols), F32),
                 pltpu.VMEM((depth + 4, tall, cols), jnp.int32),
@@ -372,19 +417,21 @@
                 pltpu.VMEM((depth + 2, tall, cols), F32),
                 pltpu.VMEM((4, depth, rows, cols), F32),
                 pltpu.VMEM((depth + 2, tall, cols), F32),
+                pltpu.VMEM((tall, cols), F32),
+                pltpu.VMEM((4, 8, 128), F32),
                 pltpu.VMEM((n * per, 8, 128), F32),
-                pltpu.VMEM((n - 1, per, 8, 128), F32),
+                pltpu.VMEM((n, per, 8, 128), F32),
                 pltpu.VMEM((8, 128), F32),
                 pltpu.VMEM((m, 8, 128), F32),
                 pltpu.VMEM((per + 1, 8, 128), F32),
                 pltpu.VMEM((n, per + 1, 8, 128), F32),
-                dma(6), dma(10), dma(10), dma(12), dma(12), dma(12), dma(12),
-                dma(n - 1), dma(n - 1), dma(m - 1), dma(m - 1), dma(n - 1), dma(n - 1),
+                dma(7), dma(12), dma(12), dma(6), dma(6), fine, fine, dma(12), dma(12),
+                dma(n), dma(n), dma(m - 1), dma(m - 1), dma(n - 1), dma(n - 1),
             ],
             compiler_params=pltpu.CompilerParams(
-                collective_id=0, has_side_effects=True, vmem_limit_bytes=48 * 1024 * 1024
+                collective_id=0, has_side_effects=True, vmem_limit_bytes=58 * 1024 * 1024
             ),
-        )(phase, solute, labels, table, heat, cotangent)
+        )(phase, solute, labels, quat_table, heat_map, cotangent)
         return final, sens, obj[0, 0]
 
     return jax.shard_map(

time: 66 us -> 57.3 us (0.87)
  starting transfers between devices: 6.42 us -> 0 us
  Pallas kernels: 45 us -> 49.3 us
  local copies, waits for them, and re-layouts: 8.15 us -> 5.34 us
  waiting for transfers between devices: 2.53 us -> 0 us
  other arithmetic: 0.9 us -> 0 us
    ppermute x2 -> x0, starting transfers between devices: 6.42 us -> none  [the longest x1 4.5 us: on_device(): lax.ppermute(heat_map[-8:], 'gy', [(i, i + 1) for i in range(m - 1)])]
    pallas_call x1, Pallas kernels: 45 us -> 49.3 us  [on_device(): pl.pallas_call(functools.partial(kernel, n, m, depth, rows, cols, per), o...]
    ppermute x2 -> x0, waiting for transfers between devices: 2.53 us -> none  [the longest x1 2.52 us: on_device(): below = lax.ppermute(heat_map[:8], 'gy', [(i + 1, i) for i in range(m - 1)])]
    unnamed x10 -> x5, local copies, waits for them, and re-layouts: 6.69 us -> 5.34 us
    concatenate x1 -> x0, other arithmetic: 0.9 us -> none  [on_device(): heat = jnp.concatenate([above, heat_map, below], 0)]
    slice x1 -> x0, local copies, waits for them, and re-layouts: 0.76 us -> none  [on_device(): heat_map[-8:]]
    pad x1 -> x0, local copies, waits for them, and re-layouts: 0.69 us -> none  [on_device(): table = jnp.pad(quat_table.T, ((0, 0), (0, 128 - grains)))]
  transfers between devices with their start and end apart: 2 -> 0, of which waited for: 1 -> 0; matrix products, arithmetic and copies ran while one was open for 1% -> 0% of each run, Pallas kernels for 0% -> 0%
where the time goes in v2:
time: 57.3 us; the launch traced here: 57 us
  Pallas kernels  49.3 us (86%)
  local copies, waits for them, and re-layouts  5.34 us (9%)
  between operations  2.4 us (4%)
    pallas_call x1, Pallas kernels, on_device(): pl.pallas_call(functools.partial(kernel, n, m, depth, rows, cols, per), o...  49.3 us
    unnamed x5, local copies, waits for them, and re-layouts  5.34 us

profile of v2, /device:TPU:1, one launch (start us, length us, event | category | flops | bytes accessed | tf_op | source)
XLA Modules:
  0.0 57.0 jit_solution(13171038659939789572)
XLA Ops:
  0.6 1.4 %copy.9.quats = f32[32,4]{1,0:T(8,128)} copy(f32[32,4]{0,1:T(4,128)} %param.9) | data formatting | bytes 1024 | tf_op args[3]
  2.0 49.3 %shard_map.85 = (f32[6,4,32,768]{3,2,1,0:T(8,128)}, f32[32,768]{1,0:T(8,128)}, f32[1,1]{1,0:T(1,128)}) custom-call(f32[4,32,768]{2,1,0:T(8,128)} %phase.1, f32[4,32,768]{2,1,0:T(8,128)} %solute.1, s32[4,32,768]{2,1,0:T(8,128)} %labels.1, f32[32,4]{1,0:T(8,128)} %copy.9.quats, f32[32,768]{1,0:T(8,128)} %heat_in.1, f32[6,4,32,768]{3,2,1,0:T(8,128)} %cot.1), custom_call_target="tpu_custom_call" | custom-call | tf_op jit(solution)/shard_map/pallas_call | solution.py:403
  51.3 0.0 copy-start
  51.3 3.3 %copy.13 = f32[6,4,32,768]{3,2,1,0:T(8,128)} copy(f32[6,4,32,768]{3,2,1,0:T(8,128)} %get-tuple-element.12) | data formatting | bytes 4718592
  54.6 0.0 copy-done
  54.6 0.6 %copy.14 = f32[32,768]{1,0:T(8,128)} copy(f32[32,768]{1,0:T(8,128)S(1)} %copy-done) | data formatting | bytes 196608
Async XLA Ops:
  51.3 3.3 %copy-start = (f32[32,768]{1,0:T(8,128)S(1)}, f32[32,768]{1,0:T(8,128)}, u32[]{:S(2)}) copy-start(f32[32,768]{1,0:T(8,128)} %get-tuple-element.13) | copy-start | bytes 294916

commit v3 on v2

--- a/solution.py
+++ b/solution.py
@@ -108,8 +108,8 @@
 
     for k in range(4):
         entry = zero
-        for grain in range(quats.shape[0]):
-            entry = jnp.where(lane == grain, quats[grain, k], entry)
+        for grain in range(quats.shape[1]):
+            entry = jnp.where(lane == grain, quats[k, grain], entry)
         table[k] = entry
     sbuf[...] = jnp.zeros_like(sbuf)
     obuf[...] = jnp.zeros_like(obuf)
@@ -431,7 +431,7 @@
             compiler_params=pltpu.CompilerParams(
                 collective_id=0, has_side_effects=True, vmem_limit_bytes=58 * 1024 * 1024
             ),
-        )(phase, solute, labels, quat_table, heat_map, cotangent)
+        )(phase, solute, labels, quat_table.T, heat_map, cotangent)
         return final, sens, obj[0, 0]
 
     return jax.shard_map(

time: 57.3 us -> 55.6 us (0.970)
  local copies, waits for them, and re-layouts: 5.34 us -> 3.98 us
    unnamed x5 -> x4, local copies, waits for them, and re-layouts: 5.34 us -> 3.98 us
where the time goes in v3:
time: 55.6 us; the launch traced here: 55.4 us
  Pallas kernels  49 us (88%)
  local copies, waits for them, and re-layouts  3.98 us (7%)
  between operations  2.4 us (4%)
    pallas_call x1, Pallas kernels, on_device(): pl.pallas_call(functools.partial(kernel, n, m, depth, rows, cols, per), o...  49 us
    unnamed x4, local copies, waits for them, and re-layouts  3.98 us

profile of v3, /device:TPU:1, one launch (start us, length us, event | category | flops | bytes accessed | tf_op | source)
XLA Modules:
  0.0 55.4 jit_solution(17947135058835607095)
XLA Ops:
  0.6 49.0 %shard_map.85 = (f32[6,4,32,768]{3,2,1,0:T(8,128)}, f32[32,768]{1,0:T(8,128)}, f32[1,1]{1,0:T(1,128)}) custom-call(f32[4,32,768]{2,1,0:T(8,128)} %phase.1, f32[4,32,768]{2,1,0:T(8,128)} %solute.1, s32[4,32,768]{2,1,0:T(8,128)} %labels.1, f32[4,32]{1,0:T(4,128)} %bitcast.2, f32[32,768]{1,0:T(8,128)} %heat_in.1, f32[6,4,32,768]{3,2,1,0:T(8,128)} %cot.1), custom_call_target="tpu_custom_call" | custom-call | tf_op jit(solution)/shard_map/pallas_call | solution.py:403
  49.7 0.0 copy-start
  49.7 3.3 %copy.12 = f32[6,4,32,768]{3,2,1,0:T(8,128)} copy(f32[6,4,32,768]{3,2,1,0:T(8,128)} %get-tuple-element.12) | data formatting | bytes 4718592
  53.0 0.0 copy-done
  53.0 0.6 %copy.13 = f32[32,768]{1,0:T(8,128)} copy(f32[32,768]{1,0:T(8,128)S(1)} %copy-done) | data formatting | bytes 196608
Async XLA Ops:
  49.7 3.3 %copy-start = (f32[32,768]{1,0:T(8,128)S(1)}, f32[32,768]{1,0:T(8,128)}, u32[]{:S(2)}) copy-start(f32[32,768]{1,0:T(8,128)} %get-tuple-element.13) | copy-start | bytes 294916
